TPU v7x, 256 devices: a whole 4x4x8 slice. The times are simulated.
256 devices in a mesh: dp: 32 (over y, z_hi, core), code: 8 (over x, z_lo).
Axes of the slice: x: 4, y: 4, z: 8 (z_hi: 4, z_lo: 2; z = z_hi * 2 + z_lo), core: 2. Of those that a mesh axis runs over, the one named last changes fastest.
Arguments:
- encoded: bfloat16 [8192, 256], P('dp'), may hold values from -32 to 32
- codebook: bfloat16 [131072, 256], P('code'), may hold values from -2 to 2
Outputs:
- grad_rows: float32 [8192, 256], P('dp')
- grad_codes: float32 [131072, 256], P(('code', 'dp'))
All inputs are finite; a program needn't handle non-finite values.
Results may differ from a plain program's by a relative error of at most 0.0045.
Values may be sent and summed in bfloat16 or wider, within the bound.
A program may use at most 64 MiB of HBM per device.

v0:
```python
import math

import jax
import jax.numpy as jnp
from jax import lax
from jax.sharding import PartitionSpec as P


def logit_block(encoded, code_rows, code_squares):
    scores = lax.dot_general(
        encoded, code_rows, (((1,), (1,)), ((), ())), preferred_element_type=jnp.float32
    )
    return scores - 0.5 * code_squares[None, :]


def grad_block(encoded, row_lse, entropy, cross_term, code_rows, code_squares, log_mass):
    logits = logit_block(encoded, code_rows, code_squares)
    weights = jnp.exp(logits - row_lse[:, None])
    shaped = weights * (
        row_lse[:, None] - logits - entropy[:, None] + log_mass[None, :] - cross_term[:, None]
    )
    return shaped.astype(jnp.bfloat16)


def code_term(grad_tile, encoded, code_rows):
    pulled = lax.dot_general(
        grad_tile, encoded, (((0,), (0,)), ((), ())), preferred_element_type=jnp.float32
    )
    totals = jnp.sum(grad_tile.astype(jnp.float32), axis=0)
    return pulled - totals[:, None] * code_rows.astype(jnp.float32)


def body(encoded, codebook):
    rows_here, features = encoded.shape
    codes_here = codebook.shape[0]
    block_size = math.gcd(codes_here, 2048)
    block_count = codes_here // block_size
    squares = jnp.sum(jnp.square(codebook.astype(jnp.float32)), axis=1)
    code_blocks = codebook.reshape(block_count, block_size, features)
    square_blocks = squares.reshape(block_count, block_size)
    row_zeros = jnp.zeros((rows_here,), jnp.float32)

    def online_step(running, inputs):
        run_max, run_sum, run_dot = running
        logits = logit_block(encoded, inputs[0], inputs[1])
        new_max = jnp.maximum(run_max, jnp.max(logits, axis=1))
        exponent = jnp.exp(logits - new_max[:, None])
        factor = jnp.exp(run_max - new_max)
        return (
            (
                new_max,
                run_sum * factor + jnp.sum(exponent, axis=1),
                run_dot * factor + jnp.sum(exponent * logits, axis=1),
            ),
            None,
        )

    start_state = (jnp.full((rows_here,), -jnp.inf, jnp.float32), row_zeros, row_zeros)
    (local_max, local_sum, local_dot), unused = lax.scan(
        online_step, start_state, (code_blocks, square_blocks)
    )
    row_max = lax.pmax(local_max, "code")
    factor = jnp.exp(local_max - row_max)
    row_sum, row_dot = lax.psum((local_sum * factor, local_dot * factor), "code")
    row_lse = row_max + jnp.log(row_sum)
    entropy = row_lse - row_dot / row_sum

    def mass_block(inputs):
        logits = logit_block(encoded, inputs[0], inputs[1])
        return jnp.sum(jnp.exp(logits - row_lse[:, None]), axis=0)

    local_mass = lax.map(mass_block, (code_blocks, square_blocks)).reshape(codes_here)
    total_rows = rows_here * lax.axis_size("dp")
    mean_mass = lax.psum(local_mass, "dp") / total_rows
    log_mass = jnp.log(mean_mass)
    log_blocks = log_mass.reshape(block_count, block_size)

    def cross_step(running, inputs):
        logits = logit_block(encoded, inputs[0], inputs[1])
        weights = jnp.exp(logits - row_lse[:, None])
        return (running + jnp.sum(weights * inputs[2][None, :], axis=1), None)

    local_cross, unused = lax.scan(cross_step, row_zeros, (code_blocks, square_blocks, log_blocks))
    cross_term = lax.psum(local_cross, "code")
    grad_start = jnp.zeros((rows_here, features), jnp.float32)

    def full_step(running, inputs):
        grad_tile = grad_block(
            encoded, row_lse, entropy, cross_term, inputs[0], inputs[1], inputs[2]
        )
        added = running + jnp.dot(grad_tile, inputs[0], preferred_element_type=jnp.float32)
        return (added, code_term(grad_tile, encoded, inputs[0]))

    local_rows, terms = lax.scan(full_step, grad_start, (code_blocks, square_blocks, log_blocks))
    grad_codes = lax.psum_scatter(
        terms.reshape(codes_here, features), "dp", scatter_dimension=0, tiled=True
    )
    grad_rows = lax.psum(local_rows, "code")
    return (grad_rows, grad_codes)


def solution(mesh):
    placed = (P("dp", None), P("code", None))
    return jax.shard_map(
        body,
        mesh=mesh,
        in_specs=placed,
        out_specs=(P("dp", None), P(("code", "dp"), None)),
        check_vma=False,
    )
```

profile of v0, /device:TPU:4, one launch (start us, length us, event | category | flops | bytes accessed | tf_op | source)
XLA Modules:
  0.0 681.3 jit_solution(13127806187103363031)
XLA Ops:
  7.3 5.2 multiply_reduce_fusion
  12.5 18.7 %while.50 = (s32[]{:T(128)}, f32[256]{0:T(256)S(1)}, f32[256]{0:T(256)S(1)}, f32[256]{0:T(256)S(1)}, bf16[8,2048,256]{2,1,0:T(8,128)(2,1)}, /*index=5*/bf16[256,...) while((s32[]{:T(128)}, f32[256]{0:T(256)S(1)}, f32[256]{0:T(256)S(1)}, ...), condition=%wide.region_5.6_spmd.clone, body=%wide.region_1.5_spmd.clone.sunk | while | flops 271585024 | bytes 5416556 | solution.py:59
  12.6 1.8 fusion.61
  14.9 1.8 fusion.61
  17.3 1.8 fusion.61
  19.6 1.8 fusion.61
  21.9 1.8 fusion.61
  24.3 1.8 fusion.61
  26.6 1.8 fusion.61
  29.0 1.8 fusion.61
  31.3 15.8 %pmax.7 = f32[256]{0:T(256)S(1)} all-reduce(f32[256]{0:T(256)S(1)} %get-tuple-element.163), channel_id=1, replica_groups=mesh['dp'=32,'code'=8] {'code'}, use_global_device_ids=true, to_apply=%region_6.7 | all-reduce | flops 256 | bytes 2048 | tf_op jit(solution)/shard_map/pmax | solution.py:62
  47.1 16.5 %psum.35 = f32[256]{0:T(256)S(1)} all-reduce(f32[256]{0:T(256)S(1)} %get-tuple-element.326), channel_id=1, replica_groups=mesh['dp'=32,'code'=8] {'code'}, use_global_device_ids=true, to_apply=%region_7.8 | all-reduce | flops 256 | bytes 2048 | tf_op jit(solution)/shard_map/psum | solution.py:64
  63.6 16.4 %while.49 = (s32[]{:T(128)}, f32[8,2048]{1,0:T(8,128)S(1)}, bf16[8,2048,256]{2,1,0:T(8,128)(2,1)}, bf16[256,256]{1,0:T(8,128)(2,1)S(1)}, f32[8,2048]{1,0:T(8,128...) while((s32[]{:T(128)}, f32[8,2048]{1,0:T(8,128)S(1)}, bf16[8,2048,256]{2,1,0:T(8,128)(2,1)}, ...), condition=%wide.region_10.11_spmd, body=%wide.region_8.10_spmd.sunk | while | flops 270008320 | bytes 1230429 | solution.py:72
  63.6 1.8 fusion.59
  65.7 1.8 fusion.59
  67.7 1.8 fusion.59
  69.8 1.8 fusion.59
  71.8 1.8 fusion.59
  73.9 1.8 fusion.59
  75.9 1.8 fusion.59
  78.0 1.8 fusion.59
  80.0 0.6 copy.4
  80.7 257.5 %all-reduce.4.cloned.1.call-done = f32[16384]{0:T(1024)} async-done(((f32[16384]{0:T(1024)}), f32[16384]{0:T(1024)}) %all-reduce.4.cloned.1.call-update) | async-done | bytes 65552 | tf_op jit(solution)/shard_map/psum | solution.py:74
  338.3 0.9 multiply_log_fusion
  339.2 15.7 %while.51 = (s32[]{:T(128)}, f32[256]{0:T(256)S(1)}, bf16[8,2048,256]{2,1,0:T(8,128)(2,1)}, bf16[256,256]{1,0:T(8,128)(2,1)S(1)}, f32[8,2048]{1,0:T(8,128)S(1)},...) while((s32[]{:T(128)}, f32[256]{0:T(256)S(1)}, ...), condition=%wide.region_15.16_spmd.clone, body=%wide.region_13.15_spmd.clone.sunk | while | flops 270534912 | bytes 1234539 | solution.py:83
  339.2 1.9 fusion.67
  341.2 1.9 fusion.67
  343.1 1.9 fusion.67
  345.1 1.9 fusion.67
  347.1 1.9 fusion.67
  349.0 1.9 fusion.67
  351.0 1.9 fusion.67
  353.0 1.9 fusion.67
  354.9 15.4 %all-reduce = (f32[256]{0:T(256)S(1)}, f32[256]{0:T(256)S(1)}) all-reduce(f32[256]{0:T(256)S(1)} %get-tuple-element.325, f32[256]{0:T(256)S(1)} %get-tuple-element.167), channel_id=1, replica_groups=mesh['dp'=32,'code'=8] {'code'}, use_global_device_ids=true, to_apply=%region_12.13 | all-reduce | flops 512 | bytes 4096 | tf_op jit(solution)/shard_map/psum | solution.py:64
  370.3 57.7 %while.52 = (s32[]{:T(128)}, f32[256,256]{1,0:T(8,128)S(1)}, f32[8,2048,256]{2,1,0:T(8,128)}, bf16[8,2048,256]{2,1,0:T(8,128)(2,1)}, bf16[256,256]{1,0:T(8,128)(...) while((s32[]{:T(128)}, f32[256,256]{1,0:T(8,128)S(1)}, ...), condition=%wide.region_19.20_spmd.clone, body=%wide.region_17.19_spmd.clone.sunk | while | flops 812253184 | bytes 9245315 | solution.py:94
  370.3 2.2 convert_reduce_fusion.2
  372.6 3.2 fusion.73
  375.8 1.7 convolution_add_fusion.2
  377.6 2.2 convert_reduce_fusion.2
  379.8 3.2 fusion.73
  383.0 1.7 convolution_add_fusion.2
  384.7 2.2 convert_reduce_fusion.2
  386.9 3.2 fusion.73
  390.2 1.7 convolution_add_fusion.2
  391.9 2.2 convert_reduce_fusion.2
  394.1 3.2 fusion.73
  397.4 1.7 convolution_add_fusion.2
  399.2 2.2 convert_reduce_fusion.2
  401.4 3.3 fusion.73
  404.7 1.7 convolution_add_fusion.2
  406.4 2.2 convert_reduce_fusion.2
  408.6 3.2 fusion.73
  411.8 1.7 convolution_add_fusion.2
  413.6 2.2 convert_reduce_fusion.2
  415.8 3.3 fusion.73
  419.1 1.7 convolution_add_fusion.2
  420.8 2.2 convert_reduce_fusion.2
  423.0 3.2 fusion.73
  426.3 1.7 convolution_add_fusion.2
  428.0 0.7 copy-done.1
  428.8 0.7 reduce-scatter.2.cloned.1.call-update
  429.5 71.3 %all-reduce.6.cloned.1.call-done = f32[256,256]{1,0:T(8,128)} async-done(((f32[256,256]{1,0:T(8,128)}), f32[256,256]{1,0:T(8,128)}) %all-reduce.6.cloned.1.call-update) | async-done | bytes 262160 | tf_op jit(solution)/shard_map/psum | solution.py:98
  500.8 172.3 %reduce-scatter.2.cloned.1.call-done = f32[512,256]{1,0:T(8,128)} async-done(((f32[16384,256]{1,0:T(8,128)}), f32[512,256]{1,0:T(8,128)}) %reduce-scatter.2.cloned.1.call-update) | async-done | bytes 524304 | tf_op jit(solution)/shard_map/reduce_scatter | solution.py:95
  673.1 1.7 copy.42
  (100 shorter events, 6.5 us)
Async XLA Ops:
  7.2 331.1 %all-reduce.4.cloned.1.call-start = ((), (), s32[]{:S(2)}) async-start(), calls=%async_computation.1 | async-start | bytes 131072 | tf_op jit(solution)/shard_map/psum | solution.py:74
  7.2 5.3 copy-start
  80.7 420.1 %all-reduce.6.cloned.1.call-start = ((), (), s32[]{:S(2)}) async-start(), calls=%async_computation.2 | async-start | bytes 524288 | tf_op jit(solution)/shard_map/psum | solution.py:98
  428.0 0.7 copy-start.1
  428.7 244.4 %reduce-scatter.2.cloned.1.call-start = ((), (), s32[]{:S(2)}) async-start(), calls=%async_computation.3 | async-start | bytes 17301504 | tf_op jit(solution)/shard_map/reduce_scatter | solution.py:95
Sparse Core Ops, SparseCore 0:
  80.8 257.4 all-reduce.3
  428.9 71.8 all-reduce.5
  505.6 167.4 reduce-scatter.1
where the time goes:
time: 683 us; the launch traced here: 681 us
  waiting for transfers between devices  502 us (73%)
  matrix products  101 us (15%)
  blocking collectives  47.7 us (7%)
  between operations  13.9 us (2%)
  other arithmetic  10.7 us (2%)
    psum x1, waiting for transfers between devices, body(): mean_mass = lax.psum(local_mass, 'dp') / total_rows  258 us
    reduce_scatter x1, waiting for transfers between devices, body(): lax.psum_scatter(terms.reshape(codes_here, features), 'dp', scatter_dimen...  172 us
    psum x1, waiting for transfers between devices, body(): grad_rows = lax.psum(local_rows, 'code')  71.3 us
    dot_general x32, matrix products, logit_block(): lax.dot_general(encoded, code_rows, (((1,), (1,)), ((), ())), preferred_e...  61.4 us
    psum x2, blocking collectives, body(): lax.psum((local_sum * factor, local_dot * factor), 'code')  31.9 us
    dot_general x8, matrix products, code_term(): lax.dot_general(grad_tile, encoded, (((0,), (0,)), ((), ())), preferred_e...  25.8 us
    pmax x1, blocking collectives, body(): row_max = lax.pmax(local_max, 'code')  15.8 us
    dot_general x8, matrix products, full_step(): jnp.dot(grad_tile, inputs[0], preferred_element_type=jnp.float32)  13.8 us
  transfers between devices with their start and end apart: 3, of which 3 were waited for; matrix products, arithmetic and copies ran while one was open for 0% of the time, Pallas kernels for 0%

commit v1 on v0

v1 whole, which is shorter than its diff:
```python
import functools

import jax
import jax.numpy as jnp
from jax import lax
from jax.experimental import pallas as pl
from jax.experimental.pallas import tpu as pltpu
from jax.sharding import PartitionSpec as P

NX, NY, NZH, NZL, NC = 4, 4, 4, 2, 2
F32, BF16 = jnp.float32, jnp.bfloat16
LANES = 128


def remote(src, dst, send_sem, recv_sem, device):
    return pltpu.make_async_remote_copy(
        src_ref=src,
        dst_ref=dst,
        send_sem=send_sem,
        recv_sem=recv_sem,
        device_id=device,
        device_id_type=pl.DeviceIdType.MESH,
    )


class Share:
    def __init__(self, buf, n, me, device_of, send_sem, recv_sem):
        self.buf, self.n, self.me, self.device_of = buf, n, me, device_of
        self.send_sem, self.recv_sem = send_sem, recv_sem

    def start(self):
        for r in range(1, self.n):
            remote(
                self.buf.at[self.me],
                self.buf.at[self.me],
                self.send_sem.at[r],
                self.recv_sem.at[self.me],
                self.device_of(lax.rem(self.me + r, self.n)),
            ).start()

    def wait_recv(self):
        for r in range(1, self.n):
            other = lax.rem(self.me + r, self.n)
            remote(
                self.buf.at[other],
                self.buf.at[other],
                self.send_sem.at[r],
                self.recv_sem.at[other],
                self.device_of(other),
            ).wait_recv()

    def wait_send(self):
        for r in range(1, self.n):
            other = lax.rem(self.me + r, self.n)
            remote(
                self.buf.at[self.me],
                self.buf.at[self.me],
                self.send_sem.at[r],
                self.recv_sem.at[self.me],
                self.device_of(other),
            ).wait_send()


def transposed(block):
    return block.astype(F32).T.astype(BF16)


def kernel(
    rows_total,
    enc, book, rows_out, codes_out,
    cbt, et, eg, ct, hsq, logit, weight, tile, lane_sum, log_mass,
    stat_x, stat_z, lse8, t8, mass, t_x, t_z,
    grad_t, row_send, row_x, row_xsum, row_xsend, row_z, row_fin,
    code_own, code_send, code_core, code_ysend, code_y,
    book_sem, es_s, es_r, ef_s, ef_r, sx_s, sx_r, sz_s, sz_r, ms_s, ms_r,
    tx_s, tx_r, tz_s, tz_r, rx_s, rx_r, rz_s, rz_r, ra_s, ra_r, rb_s, rb_r,
    cc_s, cc_r, cy_s, cy_r,
):
    rows, feats = enc.shape
    tile_rows = rows * NZH
    chunk = cbt.shape[0] // NY
    half = chunk // NC
    rb = rows // LANES
    tb = tile_rows // LANES
    nz = NZH * NZL

    dp, code = lax.axis_index("dp"), lax.axis_index("code")
    y, zh, core = dp // (NZH * NC), lax.rem(dp // NC, NZH), lax.rem(dp, NC)
    x, zl = code // NZL, lax.rem(code, NZL)
    z = zh * NZL + zl
    yc = y * NC + core

    def device(x=x, y=y, zh=zh, zl=zl, core=core):
        return ((y * NZH + zh) * NC + core, x * NZL + zl)

    def at_x(i):
        return device(x=i)

    def at_z(i):
        return device(zh=i // NZL, zl=lax.rem(i, NZL))

    def at_y(i):
        return device(y=i)

    def at_yc(i):
        return device(y=i // NC, core=lax.rem(i, NC))

    def book_copy(r, c):
        start = pl.multiple_of((c * NZH + lax.rem(zh + r, NZH)) * chunk, chunk)
        if r == 0:
            target = cbt.at[pl.ds(c * chunk, chunk), :]
        else:
            target = tile.at[pl.ds(c * chunk, chunk), pl.ds((r - 1) * feats, feats)]
        return pltpu.make_async_copy(
            book.at[pl.ds(start, chunk), :], target, book_sem.at[r * NY + c]
        )

    for r in range(NZH):
        for c in range(NY):
            book_copy(r, c).start()

    barrier = pltpu.get_barrier_semaphore()
    partners = (
        [at_x(lax.rem(x + r, NX)) for r in range(1, NX)]
        + [at_z(lax.rem(z + r, nz)) for r in range(1, nz)]
        + [at_yc(lax.rem(yc + r, NY * NC)) for r in range(1, NY * NC)]
    )
    for partner in partners:
        pl.semaphore_signal(
            barrier, inc=1, device_id=partner, device_id_type=pl.DeviceIdType.MESH
        )

    own_lanes = pl.ds(pl.multiple_of(zh * rows, LANES), rows)
    own_t = transposed(enc[...])
    et[:, own_lanes] = own_t
    eg[zh] = enc[...]

    step = 128

    def online(r, c, state):
        def body(i, state):
            top, total = state
            start = pl.multiple_of(c * chunk + i * step, step)
            if r == 0:
                codes = cbt[pl.ds(start, step), :]
            else:
                codes = tile[pl.ds(start, step), pl.ds((r - 1) * feats, feats)]
            wide = codes.astype(F32)
            squared = wide * wide
            folded = squared[:, :LANES]
            for k in range(1, feats // LANES):
                folded = folded + squared[:, k * LANES:(k + 1) * LANES]
            halved = 0.5 * jnp.sum(folded, axis=1, keepdims=True)
            if r == 0:
                hsq[pl.ds(start, step), :] = jnp.broadcast_to(halved, (step, LANES))
            scores = jnp.dot(codes, et[:, own_lanes], preferred_element_type=F32)
            logits = (scores - halved).reshape(step // 8, 8, rows)
            new_top = jnp.maximum(top, jnp.max(logits, axis=0))
            total = total * jnp.exp(top - new_top) + jnp.sum(
                jnp.exp(logits - new_top[None]), axis=0
            )
            return new_top, total

        return lax.fori_loop(0, chunk // step, body, state, unroll=True)

    slice_rows = rows // NX
    my_slice = pl.ds(pl.multiple_of(x * slice_rows, slice_rows), slice_rows)

    def e_send(r):
        other = lax.rem(zh + r, NZH)
        return remote(
            enc.at[my_slice, :], eg.at[zh, my_slice, :], es_s.at[r], es_r.at[zh], device(zh=other)
        )

    def e_recv(r):
        other = lax.rem(zh + r, NZH)
        return remote(
            enc.at[my_slice, :], eg.at[other, my_slice, :], es_s.at[r], es_r.at[other],
            device(zh=other),
        )

    def e_forward(r, q):
        other = lax.rem(zh + r, NZH)
        part = eg.at[other, my_slice, :]
        return remote(
            part, part, ef_s.at[r * NX + q], ef_r.at[other * NX + x], at_x(lax.rem(x + q, NX))
        )

    def e_forwarded(r, q):
        other, xs = lax.rem(zh + r, NZH), lax.rem(x + q, NX)
        start = pl.multiple_of(xs * slice_rows, slice_rows)
        part = eg.at[other, pl.ds(start, slice_rows), :]
        return remote(part, part, ef_s.at[r * NX + q], ef_r.at[other * NX + xs], at_x(xs))

    state = (jnp.full((8, rows), -1e30, F32), jnp.zeros((8, rows), F32))
    for r in range(NZH):
        for c in range(NY):
            book_copy(r, c).wait()

        def chunks(c, state, r=r):
            return online(r, c, state)

        state = lax.fori_loop(0, NY, chunks, state)
        if r == 0:
            pl.semaphore_wait(barrier, len(partners))
            for k in range(1, NZH):
                e_send(k).start()
    top8, total8 = state
    top = jnp.max(top8, axis=0, keepdims=True)
    total = jnp.sum(total8 * jnp.exp(top8 - top), axis=0, keepdims=True)

    for k in range(rb):
        stat_x[x, k:k + 1, :] = top[:, k * LANES:(k + 1) * LANES]
        stat_x[x, rb + k:rb + k + 1, :] = total[:, k * LANES:(k + 1) * LANES]
    share_sx = Share(stat_x, NX, x, at_x, sx_s, sx_r)
    share_sx.start()

    for r in range(1, NZH):
        e_recv(r).wait_recv()
        for q in range(1, NX):
            e_forward(r, q).start()

    mm_step = 256 if chunk % 256 == 0 else 128

    def fill_logits(block):
        lanes = pl.ds(pl.multiple_of(block * rows, LANES), rows)

        def body(i, carry):
            at = pl.ds(pl.multiple_of(i * mm_step, mm_step), mm_step)
            scores = jnp.dot(cbt[at, :], et[:, lanes], preferred_element_type=F32)
            halved = hsq[at, :]
            for k in range(rb):
                lane = pl.ds(pl.multiple_of(block * rows + k * LANES, LANES), LANES)
                logit[at, lane] = scores[:, k * LANES:(k + 1) * LANES] - halved
            return carry

        lax.fori_loop(0, NY * chunk // mm_step, body, 0, unroll=2)

    fill_logits(zh)

    share_sx.wait_recv()
    tops, sums = stat_x[:, 0:rb, :], stat_x[:, rb:2 * rb, :]
    top = jnp.max(tops, axis=0)
    stat_z[z, 0:rb, :] = top
    stat_z[z, rb:2 * rb, :] = jnp.sum(sums * jnp.exp(tops - top[None]), axis=0)
    share_sz = Share(stat_z, nz, z, at_z, sz_s, sz_r)
    share_sz.start()

    def turn_codes(i, carry):
        at = pl.ds(pl.multiple_of(i * mm_step, mm_step), mm_step)
        ct[:, at] = transposed(cbt[at, :])
        return carry

    lax.fori_loop(0, NY * chunk // mm_step, turn_codes, 0)

    for r in range(1, NZH):
        other = lax.rem(zh + r, NZH)
        for q in range(1, NX):
            e_forwarded(r, q).wait_recv()
        et[:, pl.ds(pl.multiple_of(other * rows, LANES), rows)] = transposed(eg[other])
        fill_logits(other)

    share_sz.wait_recv()
    for b in range(NZH):
        tops = stat_z[b * NZL:(b + 1) * NZL, 0:rb, :]
        sums = stat_z[b * NZL:(b + 1) * NZL, rb:2 * rb, :]
        top = jnp.max(tops, axis=0)
        lse = top + jnp.log(jnp.sum(sums * jnp.exp(tops - top[None]), axis=0))
        for k in range(rb):
            lane = (b * rb + k) * LANES
            lse8[:, lane:lane + LANES] = jnp.broadcast_to(lse[k:k + 1, :], (8, LANES))

    el_step = 32
    mass_rows = chunk // LANES
    share_m = []
    for c in range(NY):
        def weigh(i, carry, c=c):
            at = pl.ds(pl.multiple_of(c * chunk + i * el_step, el_step), el_step)
            values = logit[at, :].reshape(el_step // 8, 8, tile_rows)
            log_weights = (values - lse8[...][None]).reshape(el_step, tile_rows)
            weights = jnp.exp(log_weights)
            logit[at, :] = log_weights
            weight[at, :] = weights
            part = weights[:, :LANES]
            for k in range(1, tb):
                part = part + weights[:, k * LANES:(k + 1) * LANES]
            lane_sum[at, :] = part
            return carry

        lax.fori_loop(0, chunk // el_step, weigh, 0, unroll=2)
        for k in range(mass_rows):
            start = c * chunk + k * LANES
            mass[c, yc, k:k + 1, :] = jnp.sum(
                lane_sum[start:start + LANES, :].T, axis=0, keepdims=True
            )
        share = Share(mass.at[c], NY * NC, yc, at_yc, ms_s.at[c], ms_r.at[c])
        share.start()
        share_m.append(share)

    t_sum = jnp.zeros((8, tile_rows), F32)
    for c in range(NY):
        share_m[c].wait_recv()
        logs = jnp.log(jnp.sum(mass[c], axis=0) / rows_total)
        for k in range(mass_rows):
            start = c * chunk + k * LANES
            log_mass[start:start + LANES, :] = jnp.broadcast_to(
                logs[k:k + 1, :], (LANES, LANES)
            ).T

        def shape(i, t_sum, c=c):
            at = pl.ds(pl.multiple_of(c * chunk + i * el_step, el_step), el_step)
            logs = log_mass[at, :]
            parts = []
            for k in range(tb):
                lane = slice(k * LANES, (k + 1) * LANES)
                q = weight[at, lane] * (logs - logit[at, lane])
                logit[at, lane] = q
                parts.append(jnp.sum(q.reshape(el_step // 8, 8, LANES), axis=0))
            return t_sum + jnp.concatenate(parts, axis=1)

        t_sum = lax.fori_loop(0, chunk // el_step, shape, t_sum, unroll=2)
    t_row = jnp.sum(t_sum, axis=0, keepdims=True)
    for k in range(tb):
        t_x[x, k:k + 1, :] = t_row[:, k * LANES:(k + 1) * LANES]
    share_tx = Share(t_x, NX, x, at_x, tx_s, tx_r)
    share_tx.start()
    share_tx.wait_recv()
    t_z[z] = jnp.sum(t_x[...], axis=0)
    share_tz = Share(t_z, nz, z, at_z, tz_s, tz_r)
    share_tz.start()
    share_tz.wait_recv()
    t_all = jnp.sum(t_z[...], axis=0)
    for k in range(tb):
        t8[:, k * LANES:(k + 1) * LANES] = jnp.broadcast_to(t_all[k:k + 1, :], (8, LANES))

    grad_t[...] = jnp.zeros_like(grad_t)
    g_step = 256 if chunk % 256 == 0 else 128

    def grads(i, carry):
        at = pl.ds(pl.multiple_of(i * g_step, g_step), g_step)
        sums = jnp.zeros((g_step, LANES), F32)
        for n in range(NZH):
            parts = []
            for k in range(rb):
                lane = slice(n * rows + k * LANES, n * rows + (k + 1) * LANES)
                q = logit[at, lane].reshape(g_step // 8, 8, LANES)
                w = weight[at, lane].reshape(g_step // 8, 8, LANES)
                g = (q - w * t8[:, lane][None]).reshape(g_step, LANES)
                sums = sums + g
                parts.append(g.astype(BF16))
            block = jnp.concatenate(parts, axis=1)
            lanes = slice(n * rows, (n + 1) * rows)
            tile[at, lanes] = block
            grad_t[:, lanes] += jnp.dot(ct[:, at], block, preferred_element_type=F32)
        lane_sum[at, :] = sums
        return carry

    lax.fori_loop(0, NY * chunk // g_step, grads, 0)

    fx = feats // NX
    fz = fx // NZL
    row_send[...] = grad_t[...].astype(BF16)

    def x_part(i):
        return pl.ds(pl.multiple_of(i * fx, fx), fx)

    def row_x_copy(r, sending):
        other = lax.rem(x + r, NX)
        slot = x if sending else other
        return remote(
            row_send.at[x_part(other), :], row_x.at[slot], rx_s.at[r], rx_r.at[slot], at_x(other)
        )

    for r in range(1, NX):
        row_x_copy(r, True).start()

    partner = 1 - core

    def code_core_copy(c):
        return remote(
            code_send.at[c], code_core.at[c], cc_s.at[c], cc_r.at[c], device(core=partner)
        )

    def code_y_copy(r, sending):
        other = lax.rem(y + r, NY)
        slot = y if sending else other
        return remote(
            code_ysend.at[r], code_y.at[slot], cy_s.at[r], cy_r.at[slot], at_y(other)
        )

    def code_block(other, owner):
        start = pl.multiple_of(other * chunk + owner * half, half)
        d_step = min(half, 256)
        out = []
        for k in range(half // d_step):
            at = pl.ds(pl.multiple_of(start + k * d_step, d_step), d_step)
            pulled = jnp.dot(
                tile[at, :], eg[...].reshape(tile_rows, feats), preferred_element_type=F32
            )
            totals = jnp.sum(lane_sum[at, :], axis=1, keepdims=True)
            out.append((k * d_step, d_step, pulled - totals * cbt[at, :].astype(F32)))
        return out

    def code_compute(r):
        other = lax.rem(y + r, NY)
        for start, size, value in code_block(other, partner):
            code_send[r, start:start + size, :] = value.astype(BF16)
        code_core_copy(r).start()
        for start, size, value in code_block(other, core):
            code_own[r, start:start + size, :] = value

    def code_forward(r):
        code_core_copy(r).wait_recv()
        code_ysend[r] = (code_own[r] + code_core[r].astype(F32)).astype(BF16)
        code_y_copy(r, True).start()

    order = sorted(range(1, NY), key=lambda r: -min(r, NY - r)) + [0]
    for i, r in enumerate(order):
        code_compute(r)
        if i >= 1:
            code_forward(order[i - 1])

    for r in range(1, NX):
        row_x_copy(r, False).wait_recv()
    total = grad_t[x_part(x), :]
    for r in range(1, NX):
        total = total + row_x[lax.rem(x + r, NX)].astype(F32)
    row_xsum[...] = total
    row_xsend[...] = total.astype(BF16)

    def z_piece(i):
        return (
            pl.ds(pl.multiple_of(lax.rem(i, NZL) * fz, fz), fz),
            pl.ds(pl.multiple_of((i // NZL) * rows, LANES), rows),
        )

    def row_z_copy(r, sending):
        other = lax.rem(z + r, nz)
        slot = z if sending else other
        return remote(
            row_xsend.at[z_piece(other)], row_z.at[slot], rz_s.at[r], rz_r.at[slot], at_z(other)
        )

    for r in range(1, nz):
        row_z_copy(r, True).start()

    code_core_copy(0).wait_recv()
    codes_out[...] = code_own[0] + code_core[0].astype(F32)

    for r in range(1, nz):
        row_z_copy(r, False).wait_recv()
    total = row_xsum[z_piece(z)]
    for r in range(1, nz):
        total = total + row_z[lax.rem(z + r, nz)].astype(F32)
    row_fin[x, zl] = total

    other_zl = 1 - zl
    mine = row_fin.at[x, zl]
    remote(mine, mine, ra_s, ra_r, device(zl=other_zl)).start()
    theirs = row_fin.at[x, other_zl]
    remote(theirs, theirs, ra_s, ra_r, device(zl=other_zl)).wait_recv()
    share_rb = Share(row_fin, NX, x, at_x, rb_s, rb_r)
    share_rb.start()

    for r in range(1, NY):
        code_y_copy(r, False).wait_recv()
    total = codes_out[...]
    for r in range(1, NY):
        total = total + code_y[lax.rem(y + r, NY)].astype(F32)
    codes_out[...] = total

    share_rb.wait_recv()
    rows_out[...] = row_fin[...].reshape(feats, rows).T

    for r in range(1, NZH):
        e_send(r).wait_send()
        for q in range(1, NX):
            e_forward(r, q).wait_send()
    for share in [share_sx, share_sz, share_tx, share_tz, share_rb] + share_m:
        share.wait_send()
    for r in range(1, NX):
        row_x_copy(r, True).wait_send()
    for r in range(1, nz):
        row_z_copy(r, True).wait_send()
    remote(mine, mine, ra_s, ra_r, device(zl=other_zl)).wait_send()
    for r in range(NY):
        code_core_copy(r).wait_send()
    for r in range(1, NY):
        code_y_copy(r, True).wait_send()


def body(encoded, codebook):
    rows, feats = encoded.shape
    shard = codebook.shape[0]
    tile_codes = shard // NZH
    chunk = tile_codes // NY
    half = chunk // NC
    tile_rows = rows * NZH
    rb, tb = rows // LANES, tile_rows // LANES
    nz = NZH * NZL
    fx = feats // NX
    fz = fx // NZL
    rows_total = rows * lax.axis_size("dp")
    dma = pltpu.SemaphoreType.DMA
    scratch = [
        pltpu.VMEM((tile_codes, feats), BF16),
        pltpu.VMEM((feats, tile_rows), BF16),
        pltpu.VMEM((NZH, rows, feats), BF16),
        pltpu.VMEM((feats, tile_codes), BF16),
        pltpu.VMEM((tile_codes, LANES), F32),
        pltpu.VMEM((tile_codes, tile_rows), F32),
        pltpu.VMEM((tile_codes, tile_rows), F32),
        pltpu.VMEM((tile_codes, tile_rows), BF16),
        pltpu.VMEM((tile_codes, LANES), F32),
        pltpu.VMEM((tile_codes, LANES), F32),
        pltpu.VMEM((NX, 2 * rb, LANES), F32),
        pltpu.VMEM((nz, 2 * rb, LANES), F32),
        pltpu.VMEM((8, tile_rows), F32),
        pltpu.VMEM((8, tile_rows), F32),
        pltpu.VMEM((NY, NY * NC, chunk // LANES, LANES), F32),
        pltpu.VMEM((NX, tb, LANES), F32),
        pltpu.VMEM((nz, tb, LANES), F32),
        pltpu.VMEM((feats, tile_rows), F32),
        pltpu.VMEM((feats, tile_rows), BF16),
        pltpu.VMEM((NX, fx, tile_rows), BF16),
        pltpu.VMEM((fx, tile_rows), F32),
        pltpu.VMEM((fx, tile_rows), BF16),
        pltpu.VMEM((nz, fz, rows), BF16),
        pltpu.VMEM((NX, NZL, fz, rows), F32),
        pltpu.VMEM((NY, half, feats), F32),
        pltpu.VMEM((NY, half, feats), BF16),
        pltpu.VMEM((NY, half, feats), BF16),
        pltpu.VMEM((NY, half, feats), BF16),
        pltpu.VMEM((NY, half, feats), BF16),
        dma((NZH * NY,)),
        dma((NZH,)), dma((NZH,)), dma((NZH * NX,)), dma((NZH * NX,)),
        dma((NX,)), dma((NX,)), dma((nz,)), dma((nz,)),
        dma((NY, NY * NC)), dma((NY, NY * NC)),
        dma((NX,)), dma((NX,)), dma((nz,)), dma((nz,)),
        dma((NX,)), dma((NX,)), dma((nz,)), dma((nz,)),
        dma, dma, dma((NX,)), dma((NX,)),
        dma((NY,)), dma((NY,)), dma((NY,)), dma((NY,)),
    ]
    vmem = pl.BlockSpec(memory_space=pltpu.VMEM)
    return pl.pallas_call(
        functools.partial(kernel, float(rows_total)),
        out_shape=(
            jax.ShapeDtypeStruct((rows, feats), F32),
            jax.ShapeDtypeStruct((half, feats), F32),
        ),
        in_specs=[vmem, pl.BlockSpec(memory_space=pl.ANY)],
        out_specs=(vmem, vmem),
        scratch_shapes=scratch,
        compiler_params=pltpu.CompilerParams(
            collective_id=0, has_side_effects=True, vmem_limit_bytes=67_000_000
        ),
    )(encoded, codebook)


def solution(mesh):
    placed = (P("dp", None), P("code", None))
    return jax.shard_map(
        body,
        mesh=mesh,
        in_specs=placed,
        out_specs=(P("dp", None), P(("code", "dp"), None)),
        check_vma=False,
    )
```

time: 683 us -> 77.7 us (0.11)
  waiting for transfers between devices: 502 us -> 0 us
  matrix products: 101 us -> 0 us
  Pallas kernels: 0 us -> 72.7 us
  blocking collectives: 47.7 us -> 0 us
  between operations: 13.9 us -> 0.64 us
  other arithmetic: 10.7 us -> 0 us
    psum x2 -> x0, waiting for transfers between devices: 329 us -> none  [the longest x1 258 us: body(): mean_mass = lax.psum(local_mass, 'dp') / total_rows]
    reduce_scatter x1 -> x0, waiting for transfers between devices: 172 us -> none  [body(): lax.psum_scatter(terms.reshape(codes_here, features), 'dp', scatter_dimen...]
    dot_general x48 -> x0, matrix products: 101 us -> none  [the longest x32 61.4 us: logit_block(): lax.dot_general(encoded, code_rows, (((1,), (1,)), ((), ())), preferred_e...]
    pallas_call x0 -> x1, Pallas kernels: none -> 72.7 us  [body(): pl.pallas_call(functools.partial(kernel, float(rows_total)), out_shape=(j...]
    psum x2 -> x0, blocking collectives: 31.9 us -> none  [body(): lax.psum((local_sum * factor, local_dot * factor), 'code')]
    pmax x1 -> x0, blocking collectives: 15.8 us -> none  [body(): row_max = lax.pmax(local_max, 'code')]
    reduce_sum x9 -> x0, other arithmetic: 9.06 us -> none  [the longest x1 5.25 us: body(): squares = jnp.sum(jnp.square(codebook.astype(jnp.float32)), axis=1)]
  transfers between devices with their start and end apart: 3 -> 0, of which waited for: 3 -> 0; matrix products, arithmetic and copies ran while one was open for 0% -> 0% of each run, Pallas kernels for 0% -> 0%
where the time goes in v1:
time: 77.7 us; the launch traced here: 76.8 us
  Pallas kernels  72.7 us (94%)
  local copies, waits for them, and re-layouts  3.54 us (5%)
    pallas_call x1, Pallas kernels, body(): pl.pallas_call(functools.partial(kernel, float(rows_total)), out_shape=(j...  72.7 us
    unnamed x2, local copies, waits for them, and re-layouts  3.54 us

profile of v1, /device:TPU:4, one launch (start us, length us, event | category | flops | bytes accessed | tf_op | source)
XLA Modules:
  0.0 76.8 jit_solution(8505599289117250494)
XLA Ops:
  0.6 72.7 %shard_map.41 = (f32[256,256]{1,0:T(8,128)}, f32[512,256]{1,0:T(8,128)}) custom-call(bf16[256,256]{1,0:T(8,128)(2,1)} %enc.1, bf16[16384,256]{1,0:T(8,128)(2,1)} %book.1), custom_call_target="tpu_custom_call" | custom-call | tf_op jit(solution)/shard_map/pallas_call | solution.py:545
  73.3 1.7 %copy.6 = f32[256,256]{1,0:T(8,128)} copy(f32[256,256]{1,0:T(8,128)} %get-tuple-element.4) | data formatting | bytes 524288
  75.0 1.9 %copy.7 = f32[512,256]{1,0:T(8,128)} copy(f32[512,256]{1,0:T(8,128)} %get-tuple-element.5) | data formatting | bytes 1048576

commit v2 on v1

v2 whole, which is shorter than its diff:
```python
import functools

import jax
import jax.numpy as jnp
from jax import lax
from jax.experimental import pallas as pl
from jax.experimental.pallas import tpu as pltpu
from jax.sharding import PartitionSpec as P

NX, NY, NZH, NZL, NC = 4, 4, 4, 2, 2
F32, BF16 = jnp.float32, jnp.bfloat16
LANES = 128


def remote(src, dst, send_sem, recv_sem, device):
    return pltpu.make_async_remote_copy(
        src_ref=src,
        dst_ref=dst,
        send_sem=send_sem,
        recv_sem=recv_sem,
        device_id=device,
        device_id_type=pl.DeviceIdType.MESH,
    )


class Copy:
    def __init__(self, log, outgoing, incoming):
        self.outgoing, self.incoming, self.arrived = outgoing, incoming, False
        outgoing.start()
        log.append(self)

    def recv(self):
        self.incoming.wait_recv()
        self.arrived = True

    def finish(self):
        if not self.arrived:
            self.recv()
        self.outgoing.wait_send()


class Share:
    def __init__(self, log, buf, n, me, device_of, send_sem, recv_sem):
        self.copies = []
        for r in range(1, n):
            there = lax.rem(me + r, n)

            def slot(i, r=r, there=there):
                return remote(
                    buf.at[i], buf.at[i], send_sem.at[r], recv_sem.at[i], device_of(there)
                )

            self.copies.append(Copy(log, slot(me), slot(there)))

    def recv(self):
        for copy in self.copies:
            copy.recv()


def transposed(block):
    return block.astype(F32).T.astype(BF16)


def kernel(
    rows_total,
    enc, book, rows_out, codes_out,
    cbt, et, eg, ct, hsq, logit, weight, tile, lane_sum, log_mass,
    stat_x, stat_z, lse8, t8, mass, t_x, t_z,
    grad_t, row_send, row_x, row_xsend, row_z, row_fin,
    code_own, code_send, code_core, code_ysend, code_y,
    book_sem, es_s, es_r, ef_s, ef_r, sx_s, sx_r, sz_s, sz_r, ms_s, ms_r,
    tx_s, tx_r, tz_s, tz_r, rx_s, rx_r, rz_s, rz_r, rb_s, rb_r,
    cc_s, cc_r, cy_s, cy_r,
):
    rows, feats = enc.shape
    tile_rows = rows * NZH
    chunk = cbt.shape[0] // NY
    half = chunk // NC
    rb = rows // LANES
    tb = tile_rows // LANES
    nz = NZH * NZL

    dp, code = lax.axis_index("dp"), lax.axis_index("code")
    y, zh, core = dp // (NZH * NC), lax.rem(dp // NC, NZH), lax.rem(dp, NC)
    x, zl = code // NZL, lax.rem(code, NZL)
    z = zh * NZL + zl
    yc = y * NC + core

    def device(x=x, y=y, zh=zh, zl=zl, core=core):
        return ((y * NZH + zh) * NC + core, x * NZL + zl)

    def at_x(i):
        return device(x=i)

    def at_z(i):
        return device(zh=i // NZL, zl=lax.rem(i, NZL))

    def at_y(i):
        return device(y=i)

    def at_xl(i):
        return device(x=i // NZL, zl=lax.rem(i, NZL))

    def at_yc(i):
        return device(y=i // NC, core=lax.rem(i, NC))

    def book_copy(r, c):
        start = pl.multiple_of((c * NZH + lax.rem(zh + r, NZH)) * chunk, chunk)
        if r == 0:
            target = cbt.at[pl.ds(c * chunk, chunk), :]
        else:
            target = tile.at[pl.ds(c * chunk, chunk), pl.ds((r - 1) * feats, feats)]
        return pltpu.make_async_copy(
            book.at[pl.ds(start, chunk), :], target, book_sem.at[r * NY + c]
        )

    for r in range(NZH):
        for c in range(NY):
            book_copy(r, c).start()

    log = []

    barrier = pltpu.get_barrier_semaphore()
    partners = (
        [at_x(lax.rem(x + r, NX)) for r in range(1, NX)]
        + [at_z(lax.rem(z + r, nz)) for r in range(1, nz)]
        + [at_yc(lax.rem(yc + r, NY * NC)) for r in range(1, NY * NC)]
        + [device(x=lax.rem(x + r, NX), zl=1 - zl) for r in range(1, NX)]
    )
    for partner in partners:
        pl.semaphore_signal(
            barrier, inc=1, device_id=partner, device_id_type=pl.DeviceIdType.MESH
        )

    own_lanes = pl.ds(pl.multiple_of(zh * rows, LANES), rows)
    own_t = transposed(enc[...])
    et[:, own_lanes] = own_t
    eg[zh] = enc[...]

    step = 128

    def online(r, c, state):
        def body(i, state):
            top, total = state
            start = pl.multiple_of(c * chunk + i * step, step)
            if r == 0:
                codes = cbt[pl.ds(start, step), :]
            else:
                codes = tile[pl.ds(start, step), pl.ds((r - 1) * feats, feats)]
            wide = codes.astype(F32)
            squared = wide * wide
            folded = squared[:, :LANES]
            for k in range(1, feats // LANES):
                folded = folded + squared[:, k * LANES:(k + 1) * LANES]
            halved = 0.5 * jnp.sum(folded, axis=1, keepdims=True)
            if r == 0:
                hsq[pl.ds(start, step), :] = jnp.broadcast_to(halved, (step, LANES))
            scores = jnp.dot(codes, et[:, own_lanes], preferred_element_type=F32)
            logits = (scores - halved).reshape(step // 8, 8, rows)
            new_top = jnp.maximum(top, jnp.max(logits, axis=0))
            total = total * jnp.exp(top - new_top) + jnp.sum(
                jnp.exp(logits - new_top[None]), axis=0
            )
            return new_top, total

        return lax.fori_loop(0, chunk // step, body, state, unroll=True)

    slice_rows = rows // NX
    my_slice = pl.ds(pl.multiple_of(x * slice_rows, slice_rows), slice_rows)

    def e_copy(r):
        other = lax.rem(zh + r, NZH)

        def slot(i):
            return remote(
                enc.at[my_slice, :], eg.at[i, my_slice, :], es_s.at[r], es_r.at[i], device(zh=other)
            )

        return Copy(log, slot(zh), slot(other))

    def e_forward(r, q):
        other, xs = lax.rem(zh + r, NZH), lax.rem(x + q, NX)
        theirs = pl.ds(pl.multiple_of(xs * slice_rows, slice_rows), slice_rows)

        def slot(i, part):
            return remote(
                eg.at[other, part, :], eg.at[other, part, :], ef_s.at[r * NX + q],
                ef_r.at[other * NX + i], at_x(xs),
            )

        return Copy(log, slot(x, my_slice), slot(xs, theirs))

    state = (jnp.full((8, rows), -1e30, F32), jnp.zeros((8, rows), F32))
    near_first = sorted(range(1, NZH), key=lambda r: min(r, NZH - r))
    e_first = {}
    for r in range(NZH):
        if r == NZH - 1:
            pl.semaphore_wait(barrier, len(partners))
            e_first = {r: e_copy(r) for r in near_first}
        for c in range(NY):
            book_copy(r, c).wait()

        def chunks(c, state, r=r):
            return online(r, c, state)

        state = lax.fori_loop(0, NY, chunks, state)
    top8, total8 = state
    top = jnp.max(top8, axis=0, keepdims=True)
    total = jnp.sum(total8 * jnp.exp(top8 - top), axis=0, keepdims=True)

    for k in range(rb):
        stat_x[x, k:k + 1, :] = top[:, k * LANES:(k + 1) * LANES]
        stat_x[x, rb + k:rb + k + 1, :] = total[:, k * LANES:(k + 1) * LANES]
    share_sx = Share(log, stat_x, NX, x, at_x, sx_s, sx_r)


    mm_step = min(NY * chunk, 1024)

    def fill_logits(block):
        lanes = pl.ds(pl.multiple_of(block * rows, LANES), rows)

        def body(i, carry):
            at = pl.ds(pl.multiple_of(i * mm_step, mm_step), mm_step)
            scores = jnp.dot(cbt[at, :], et[:, lanes], preferred_element_type=F32)
            halved = hsq[at, :]
            for k in range(rb):
                lane = pl.ds(pl.multiple_of(block * rows + k * LANES, LANES), LANES)
                logit[at, lane] = scores[:, k * LANES:(k + 1) * LANES] - halved
            return carry

        lax.fori_loop(0, NY * chunk // mm_step, body, 0)

    fill_logits(zh)

    e_second = {}
    for r in near_first:
        e_first[r].recv()
        e_second[r] = [e_forward(r, q) for q in range(1, NX)]

    share_sx.recv()
    tops, sums = stat_x[:, 0:rb, :], stat_x[:, rb:2 * rb, :]
    top = jnp.max(tops, axis=0)
    stat_z[z, 0:rb, :] = top
    stat_z[z, rb:2 * rb, :] = jnp.sum(sums * jnp.exp(tops - top[None]), axis=0)
    share_sz = Share(log, stat_z, nz, z, at_z, sz_s, sz_r)

    for r in near_first:
        other = lax.rem(zh + r, NZH)
        for copy in e_second[r]:
            copy.recv()
        et[:, pl.ds(pl.multiple_of(other * rows, LANES), rows)] = transposed(eg[other])
        fill_logits(other)

    share_sz.recv()
    for b in range(NZH):
        tops = stat_z[b * NZL:(b + 1) * NZL, 0:rb, :]
        sums = stat_z[b * NZL:(b + 1) * NZL, rb:2 * rb, :]
        top = jnp.max(tops, axis=0)
        lse = top + jnp.log(jnp.sum(sums * jnp.exp(tops - top[None]), axis=0))
        for k in range(rb):
            lane = (b * rb + k) * LANES
            lse8[:, lane:lane + LANES] = jnp.broadcast_to(lse[k:k + 1, :], (8, LANES))

    el_step = 64
    mass_rows = chunk // LANES
    share_m = []
    for c in range(NY):
        def weigh(i, carry, c=c):
            at = pl.ds(pl.multiple_of(c * chunk + i * el_step, el_step), el_step)
            part = None
            for k in range(tb):
                lane = slice(k * LANES, (k + 1) * LANES)
                values = logit[at, lane].reshape(el_step // 8, 8, LANES)
                log_weights = (values - lse8[:, lane][None]).reshape(el_step, LANES)
                weights = jnp.exp(log_weights)
                logit[at, lane] = log_weights
                weight[at, lane] = weights
                part = weights if part is None else part + weights
            lane_sum[at, :] = part
            return carry

        lax.fori_loop(0, chunk // el_step, weigh, 0, unroll=2)
        for k in range(mass_rows):
            start = c * chunk + k * LANES
            mass[c, yc, k:k + 1, :] = jnp.sum(
                lane_sum[start:start + LANES, :].T, axis=0, keepdims=True
            )
        share_m.append(Share(log, mass.at[c], NY * NC, yc, at_yc, ms_s.at[c], ms_r.at[c]))

    t_sum = jnp.zeros((8, tile_rows), F32)
    for c in range(NY):
        share_m[c].recv()
        logs = jnp.log(jnp.sum(mass[c], axis=0) / rows_total)
        for k in range(mass_rows):
            start = c * chunk + k * LANES
            log_mass[start:start + LANES, :] = jnp.broadcast_to(
                logs[k:k + 1, :], (LANES, LANES)
            ).T

        def shape(i, t_sum, c=c):
            at = pl.ds(pl.multiple_of(c * chunk + i * el_step, el_step), el_step)
            logs = log_mass[at, :]
            parts = []
            for k in range(tb):
                lane = slice(k * LANES, (k + 1) * LANES)
                q = weight[at, lane] * (logs - logit[at, lane])
                logit[at, lane] = q
                parts.append(jnp.sum(q.reshape(el_step // 8, 8, LANES), axis=0))
            return t_sum + jnp.concatenate(parts, axis=1)

        t_sum = lax.fori_loop(0, chunk // el_step, shape, t_sum, unroll=2)
    t_row = jnp.sum(t_sum, axis=0, keepdims=True)
    for k in range(tb):
        t_x[x, k:k + 1, :] = t_row[:, k * LANES:(k + 1) * LANES]
    share_tx = Share(log, t_x, NX, x, at_x, tx_s, tx_r)

    turn_step = min(NY * chunk, 256)

    def turn_codes(i, carry):
        at = pl.ds(pl.multiple_of(i * turn_step, turn_step), turn_step)
        ct[:, at] = transposed(cbt[at, :])
        return carry

    lax.fori_loop(0, NY * chunk // turn_step, turn_codes, 0)

    share_tx.recv()
    t_z[z] = jnp.sum(t_x[...], axis=0)
    Share(log, t_z, nz, z, at_z, tz_s, tz_r).recv()
    t_all = jnp.sum(t_z[...], axis=0)
    for k in range(tb):
        t8[:, k * LANES:(k + 1) * LANES] = jnp.broadcast_to(t_all[k:k + 1, :], (8, LANES))

    partner = 1 - core
    g_step = min(half, 256)

    def grad_tile(start):
        at = pl.ds(start, g_step)
        sums = jnp.zeros((g_step, LANES), F32)
        for k in range(tb):
            lane = slice(k * LANES, (k + 1) * LANES)
            q = logit[at, lane].reshape(g_step // 8, 8, LANES)
            w = weight[at, lane].reshape(g_step // 8, 8, LANES)
            g = (q - w * t8[:, lane][None]).reshape(g_step, LANES)
            sums = sums + g
            tile[at, lane] = g.astype(BF16)
        lane_sum[at, :] = sums

    def code_grad(start):
        at = pl.ds(start, g_step)
        totals = jnp.sum(lane_sum[at, :], axis=1, keepdims=True)
        pulled = jnp.dot(
            tile[at, :], eg[...].reshape(tile_rows, feats), preferred_element_type=F32
        )
        return pulled - totals * cbt[at, :].astype(F32)

    def code_compute(r, fill, multiply):
        first = lax.rem(y + r, NY) * chunk

        def body(k, carry):
            theirs = pl.multiple_of(first + partner * half + k * g_step, g_step)
            ours = pl.multiple_of(first + core * half + k * g_step, g_step)
            to = pl.ds(pl.multiple_of(k * g_step, g_step), g_step)
            if fill:
                grad_tile(theirs)
            if multiply:
                code_send[r, to, :] = code_grad(theirs).astype(BF16)
            if fill:
                grad_tile(ours)
            if multiply:
                code_own[r, to, :] = code_grad(ours)
            return carry

        lax.fori_loop(0, half // g_step, body, 0)

    def code_exchange(r):
        copy = remote(
            code_send.at[r], code_core.at[r], cc_s.at[r], cc_r.at[r], device(core=partner)
        )
        return Copy(log, copy, copy)

    def code_forward(r):
        core_copies[r].recv()
        code_ysend[r] = (code_own[r] + code_core[r].astype(F32)).astype(BF16)
        other = lax.rem(y + r, NY)

        def slot(i):
            return remote(
                code_ysend.at[r], code_y.at[i], cy_s.at[r], cy_r.at[i], at_y(other)
            )

        return Copy(log, slot(y), slot(other))

    far_first = sorted(range(1, NY), key=lambda r: -min(r, NY - r)) + [0]
    core_copies, y_copies = {}, {}
    for i, r in enumerate(far_first):
        code_compute(r, True, r != 0)
        if r:
            core_copies[r] = code_exchange(r)
        if i >= 1:
            y_copies[far_first[i - 1]] = code_forward(far_first[i - 1])

    fx = feats // NX
    x_slice = pl.ds(pl.multiple_of(x * fx, fx), fx)

    def row_compute(r):
        lanes = pl.ds(pl.multiple_of(lax.rem(zh + r, NZH) * rows, LANES), rows)
        value = jnp.dot(ct[...], tile[:, lanes], preferred_element_type=F32)
        grad_t[r] = value
        row_send[r] = value.astype(BF16)
        copies = []
        for q in range(1, NX):
            other = lax.rem(x + q, NX)

            def slot(i, q=q, other=other):
                part = pl.ds(pl.multiple_of(other * fx, fx), fx)
                return remote(
                    row_send.at[r, part, :], row_x.at[i, r], rx_s.at[r, q], rx_r.at[r, i],
                    at_x(other),
                )

            copies.append(Copy(log, slot(x), slot(other)))
        return copies

    def row_forward(r):
        for copy in x_copies[r]:
            copy.recv()
        total = grad_t[r, x_slice, :]
        for q in range(1, NX):
            total = total + row_x[lax.rem(x + q, NX), r].astype(F32)
        if r == 0:
            return total
        row_xsend[r] = total.astype(BF16)
        other = lax.rem(zh + r, NZH)

        def slot(i):
            return remote(row_xsend.at[r], row_z.at[i], rz_s.at[r], rz_r.at[i], device(zh=other))

        z_copies.append(Copy(log, slot(zh), slot(other)))

    far_blocks = sorted(range(1, NZH), key=lambda r: -min(r, NZH - r)) + [0]
    x_copies, z_copies = {}, []
    for i, r in enumerate(far_blocks):
        x_copies[r] = row_compute(r)
        if i >= 2:
            row_forward(far_blocks[i - 2])
    code_compute(0, False, True)
    core_copies[0] = code_exchange(0)
    row_forward(far_blocks[-2])
    total = row_forward(far_blocks[-1])
    for copy in z_copies:
        copy.recv()
    for r in range(1, NZH):
        total = total + row_z[lax.rem(zh + r, NZH)].astype(F32)
    slot = x * NZL + zl
    row_fin[slot] = total.astype(BF16)
    share_rb = Share(log, row_fin, NX * NZL, slot, at_xl, rb_s, rb_r)

    core_copies[0].recv()
    codes_out[...] = code_own[0] + code_core[0].astype(F32)
    for r in far_first[:-1]:
        y_copies[r].recv()
        codes_out[...] += code_y[lax.rem(y + r, NY)].astype(F32)

    share_rb.recv()
    for k in range(NX):
        part = row_fin[k * NZL].astype(F32)
        for j in range(1, NZL):
            part = part + row_fin[k * NZL + j].astype(F32)
        rows_out[:, k * fx:(k + 1) * fx] = part.T

    for copy in log:
        copy.finish()


def body(encoded, codebook):
    rows, feats = encoded.shape
    shard = codebook.shape[0]
    tile_codes = shard // NZH
    chunk = tile_codes // NY
    half = chunk // NC
    tile_rows = rows * NZH
    rb, tb = rows // LANES, tile_rows // LANES
    nz = NZH * NZL
    fx = feats // NX
    rows_total = rows * lax.axis_size("dp")
    dma = pltpu.SemaphoreType.DMA
    scratch = [
        pltpu.VMEM((tile_codes, feats), BF16),
        pltpu.VMEM((feats, tile_rows), BF16),
        pltpu.VMEM((NZH, rows, feats), BF16),
        pltpu.VMEM((feats, tile_codes), BF16),
        pltpu.VMEM((tile_codes, LANES), F32),
        pltpu.VMEM((tile_codes, tile_rows), F32),
        pltpu.VMEM((tile_codes, tile_rows), F32),
        pltpu.VMEM((tile_codes, tile_rows), BF16),
        pltpu.VMEM((tile_codes, LANES), F32),
        pltpu.VMEM((tile_codes, LANES), F32),
        pltpu.VMEM((NX, 2 * rb, LANES), F32),
        pltpu.VMEM((nz, 2 * rb, LANES), F32),
        pltpu.VMEM((8, tile_rows), F32),
        pltpu.VMEM((8, tile_rows), F32),
        pltpu.VMEM((NY, NY * NC, chunk // LANES, LANES), F32),
        pltpu.VMEM((NX, tb, LANES), F32),
        pltpu.VMEM((nz, tb, LANES), F32),
        pltpu.VMEM((NZH, feats, rows), F32),
        pltpu.VMEM((NZH, feats, rows), BF16),
        pltpu.VMEM((NX, NZH, fx, rows), BF16),
        pltpu.VMEM((NZH, fx, rows), BF16),
        pltpu.VMEM((NZH, fx, rows), BF16),
        pltpu.VMEM((NX * NZL, fx, rows), BF16),
        pltpu.VMEM((NY, half, feats), F32),
        pltpu.VMEM((NY, half, feats), BF16),
        pltpu.VMEM((NY, half, feats), BF16),
        pltpu.VMEM((NY, half, feats), BF16),
        pltpu.VMEM((NY, half, feats), BF16),
        dma((NZH * NY,)),
        dma((NZH,)), dma((NZH,)), dma((NZH * NX,)), dma((NZH * NX,)),
        dma((NX,)), dma((NX,)), dma((nz,)), dma((nz,)),
        dma((NY, NY * NC)), dma((NY, NY * NC)),
        dma((NX,)), dma((NX,)), dma((nz,)), dma((nz,)),
        dma((NZH, NX)), dma((NZH, NX)), dma((NZH,)), dma((NZH,)),
        dma((NX * NZL,)), dma((NX * NZL,)),
        dma((NY,)), dma((NY,)), dma((NY,)), dma((NY,)),
    ]
    vmem = pl.BlockSpec(memory_space=pltpu.VMEM)
    return pl.pallas_call(
        functools.partial(kernel, float(rows_total)),
        out_shape=(
            jax.ShapeDtypeStruct((rows, feats), F32),
            jax.ShapeDtypeStruct((half, feats), F32),
        ),
        in_specs=[vmem, pl.BlockSpec(memory_space=pl.ANY)],
        out_specs=(vmem, vmem),
        scratch_shapes=scratch,
        compiler_params=pltpu.CompilerParams(
            collective_id=0, has_side_effects=True, vmem_limit_bytes=67_000_000
        ),
    )(encoded, codebook)


def solution(mesh):
    placed = (P("dp", None), P("code", None))
    return jax.shard_map(
        body,
        mesh=mesh,
        in_specs=placed,
        out_specs=(P("dp", None), P(("code", "dp"), None)),
        check_vma=False,
    )
```

time: 77.7 us -> 76 us (0.978)
  Pallas kernels: 72.7 us -> 70.5 us
    pallas_call x1, Pallas kernels: 72.7 us -> 70.5 us  [body(): pl.pallas_call(functools.partial(kernel, float(rows_total)), out_shape=(j...]
where the time goes in v2:
time: 76 us; the launch traced here: 74.7 us
  Pallas kernels  70.5 us (93%)
  local copies, waits for them, and re-layouts  3.54 us (5%)
    pallas_call x1, Pallas kernels, body(): pl.pallas_call(functools.partial(kernel, float(rows_total)), out_shape=(j...  70.5 us
    unnamed x2, local copies, waits for them, and re-layouts  3.54 us

profile of v2, /device:TPU:4, one launch (start us, length us, event | category | flops | bytes accessed | tf_op | source)
XLA Modules:
  0.0 74.7 jit_solution(16189875616853551309)
XLA Ops:
  0.6 70.5 %shard_map.41 = (f32[256,256]{1,0:T(8,128)}, f32[512,256]{1,0:T(8,128)}) custom-call(bf16[256,256]{1,0:T(8,128)(2,1)} %enc.1, bf16[16384,256]{1,0:T(8,128)(2,1)} %book.1), custom_call_target="tpu_custom_call" | custom-call | tf_op jit(solution)/shard_map/pallas_call | solution.py:526
  71.1 1.7 %copy.6 = f32[256,256]{1,0:T(8,128)} copy(f32[256,256]{1,0:T(8,128)} %get-tuple-element.4) | data formatting | bytes 524288
  72.8 1.9 %copy.7 = f32[512,256]{1,0:T(8,128)} copy(f32[512,256]{1,0:T(8,128)} %get-tuple-element.5) | data formatting | bytes 1048576

commit v3 on v2

--- a/solution.py
+++ b/solution.py
@@ -114,9 +114,8 @@
             book.at[pl.ds(start, chunk), :], target, book_sem.at[r * NY + c]
         )
 
-    for r in range(NZH):
-        for c in range(NY):
-            book_copy(r, c).start()
+    for c in range(NY):
+        book_copy(0, c).start()
 
     log = []
 
@@ -170,10 +169,11 @@
 
     def e_copy(r):
         other = lax.rem(zh + r, NZH)
+        part = my_slice if 2 * r == NZH else pl.ds(0, rows)
 
         def slot(i):
             return remote(
-                enc.at[my_slice, :], eg.at[i, my_slice, :], es_s.at[r], es_r.at[i], device(zh=other)
+                enc.at[part, :], eg.at[i, part, :], es_s.at[r], es_r.at[i], device(zh=other)
             )
 
         return Copy(log, slot(zh), slot(other))
@@ -191,14 +191,17 @@
         return Copy(log, slot(x, my_slice), slot(xs, theirs))
 
     state = (jnp.full((8, rows), -1e30, F32), jnp.zeros((8, rows), F32))
-    near_first = sorted(range(1, NZH), key=lambda r: min(r, NZH - r))
+    far_then_near = sorted(range(1, NZH), key=lambda r: -min(r, NZH - r))
+    far_rows = far_then_near[0]
     e_first = {}
     for r in range(NZH):
         if r == NZH - 1:
             pl.semaphore_wait(barrier, len(partners))
-            e_first = {r: e_copy(r) for r in near_first}
+            e_first = {k: e_copy(k) for k in far_then_near}
         for c in range(NY):
             book_copy(r, c).wait()
+        for c in range(NY if r < NZH - 1 else 0):
+            book_copy(r + 1, c).start()
 
         def chunks(c, state, r=r):
             return online(r, c, state)
@@ -232,10 +235,8 @@
 
     fill_logits(zh)
 
-    e_second = {}
-    for r in near_first:
-        e_first[r].recv()
-        e_second[r] = [e_forward(r, q) for q in range(1, NX)]
+    e_first[far_rows].recv()
+    e_second = [e_forward(far_rows, q) for q in range(1, NX)]
 
     share_sx.recv()
     tops, sums = stat_x[:, 0:rb, :], stat_x[:, rb:2 * rb, :]
@@ -244,9 +245,9 @@
     stat_z[z, rb:2 * rb, :] = jnp.sum(sums * jnp.exp(tops - top[None]), axis=0)
     share_sz = Share(log, stat_z, nz, z, at_z, sz_s, sz_r)
 
-    for r in near_first:
+    for r in far_then_near[1:] + [far_rows]:
         other = lax.rem(zh + r, NZH)
-        for copy in e_second[r]:
+        for copy in e_second if r == far_rows else [e_first[r]]:
             copy.recv()
         et[:, pl.ds(pl.multiple_of(other * rows, LANES), rows)] = transposed(eg[other])
         fill_logits(other)
@@ -392,12 +393,6 @@
 
     far_first = sorted(range(1, NY), key=lambda r: -min(r, NY - r)) + [0]
     core_copies, y_copies = {}, {}
-    for i, r in enumerate(far_first):
-        code_compute(r, True, r != 0)
-        if r:
-            core_copies[r] = code_exchange(r)
-        if i >= 1:
-            y_copies[far_first[i - 1]] = code_forward(far_first[i - 1])
 
     fx = feats // NX
     x_slice = pl.ds(pl.multiple_of(x * fx, fx), fx)
@@ -439,10 +434,27 @@
 
     far_blocks = sorted(range(1, NZH), key=lambda r: -min(r, NZH - r)) + [0]
     x_copies, z_copies = {}, []
+    early, late = far_first[:-1][:2], far_first[:-1][2:]
+    for i, r in enumerate(early):
+        code_compute(r, True, True)
+        core_copies[r] = code_exchange(r)
+        if i >= 1:
+            y_copies[early[i - 1]] = code_forward(early[i - 1])
+    for r in late + [0]:
+        code_compute(r, True, False)
     for i, r in enumerate(far_blocks):
         x_copies[r] = row_compute(r)
+        if i == 0:
+            y_copies[early[-1]] = code_forward(early[-1])
+        if i == 1:
+            for k in late:
+                code_compute(k, False, True)
+                core_copies[k] = code_exchange(k)
         if i >= 2:
             row_forward(far_blocks[i - 2])
+        if i == 2:
+            for k in late:
+                y_copies[k] = code_forward(k)
     code_compute(0, False, True)
     core_copies[0] = code_exchange(0)
     row_forward(far_blocks[-2])
@@ -470,6 +482,11 @@
 
     for copy in log:
         copy.finish()
+
+
+def hand_over(rows_in, codes_in, rows_out, codes_out):
+    rows_out[...] = rows_in[...]
+    codes_out[...] = codes_in[...]
 
 
 def body(encoded, codebook):
@@ -523,12 +540,13 @@
         dma((NY,)), dma((NY,)), dma((NY,)), dma((NY,)),
     ]
     vmem = pl.BlockSpec(memory_space=pltpu.VMEM)
-    return pl.pallas_call(
+    shapes = (
+        jax.ShapeDtypeStruct((rows, feats), F32),
+        jax.ShapeDtypeStruct((half, feats), F32),
+    )
+    results = pl.pallas_call(
         functools.partial(kernel, float(rows_total)),
-        out_shape=(
-            jax.ShapeDtypeStruct((rows, feats), F32),
-            jax.ShapeDtypeStruct((half, feats), F32),
-        ),
+        out_shape=shapes,
         in_specs=[vmem, pl.BlockSpec(memory_space=pl.ANY)],
         out_specs=(vmem, vmem),
         scratch_shapes=scratch,
@@ -536,6 +554,9 @@
             collective_id=0, has_side_effects=True, vmem_limit_bytes=67_000_000
         ),
     )(encoded, codebook)
+    return pl.pallas_call(
+        hand_over, out_shape=shapes, in_specs=[vmem, vmem], out_specs=(vmem, vmem)
+    )(*results)
 
 
 def solution(mesh):

time: 76 us -> 73.8 us (0.971)
  local copies, waits for them, and re-layouts: 3.54 us -> 0 us
  Pallas kernels: 70.5 us -> 72.2 us
    unnamed x2 -> x0, local copies, waits for them, and re-layouts: 3.54 us -> none
    pallas_call x1 -> x2, Pallas kernels: 70.5 us -> 72.2 us  [the longest x1 70.2 us: body(): pl.pallas_call(functools.partial(kernel, float(rows_total)), out_shape=sh...]
where the time goes in v3:
time: 73.8 us; the launch traced here: 72.8 us
  Pallas kernels  72.2 us (98%)
    pallas_call x1, Pallas kernels, body(): pl.pallas_call(functools.partial(kernel, float(rows_total)), out_shape=sh...  70.2 us
    pallas_call x1, Pallas kernels, body(): pl.pallas_call(hand_over, out_shape=shapes, in_specs=[vmem, vmem], out_sp...  2.02 us

profile of v3, /device:TPU:4, one launch (start us, length us, event | category | flops | bytes accessed | tf_op | source)
XLA Modules:
  0.0 72.8 jit_solution(4673089809410891822)
XLA Ops:
  0.6 70.2 %shard_map.41 = (f32[256,256]{1,0:T(8,128)}, f32[512,256]{1,0:T(8,128)}) custom-call(bf16[256,256]{1,0:T(8,128)(2,1)} %enc.1, bf16[16384,256]{1,0:T(8,128)(2,1)} %book.1), custom_call_target="tpu_custom_call" | custom-call | tf_op jit(solution)/shard_map/pallas_call | solution.py:547
  70.8 2.0 %shard_map.42 = (f32[256,256]{1,0:T(8,128)}, f32[512,256]{1,0:T(8,128)}) custom-call(f32[256,256]{1,0:T(8,128)} %get-tuple-element.4.rows_in, f32[512,256]{1,0:T(8,128)} %get-tuple-element.5.codes_in), custom_call_target="tpu_custom_call" | custom-call | tf_op jit(solution)/shard_map/pallas_call | solution.py:557
